TPU v7x, 32 devices: a whole 2x2x4 slice. The times are simulated.
32 devices in a mesh: energy: 8 (over z, x), slab: 4 (over y, core).
Axes of the slice: x: 2, y: 2, z: 4, core: 2. Of those that a mesh axis runs over, the one named last changes fastest.
Arguments:
- green: bfloat16 [256, 4608], P('energy', 'slab'), may hold values from -1.75 to 1.75
- sigma_in: bfloat16 [256, 4608], P('energy', 'slab'), may hold values from -6 to 6
- neighbours: int32 [32, 8], P('slab'), may hold values from 0 to 11
- coupling: float32 [32, 8], P('slab'), may hold values from 0.1 to 1
- send_down: int32 [4, 2], P('slab'), may hold values from 0 to 7, as said below
- send_up: int32 [4, 2], P('slab'), may hold values from 0 to 7, as said below
- offsets: int32 [16], replicated, may hold values from 1 to 32, as said below
- w_emit: float32 [16], replicated, may hold values from 0.02 to 0.2
- w_absorb: float32 [16], replicated, may hold values from 0.02 to 0.2
Outputs:
- sigma_ph: bfloat16 [256, 4608], P('energy', 'slab')
- g_less: bfloat16 [256, 4608], P('energy', 'slab')
Inputs may be any that keep to these rules, and one draw needn't show every extreme that they name: Each row of send_down holds 2 distinct atom numbers of one slab. Each row of send_up holds 2 distinct atom numbers of one slab. The 16 offsets are distinct, and 32 is one of them.
All inputs are finite; a program needn't handle non-finite values.
Results may differ from a plain program's by a relative error of at most 0.0063.
Values may be sent and summed in bfloat16 or wider, within the bound.
A program may use at most 128 MiB of HBM per device.

v0:
```python
import functools

import jax
import jax.numpy as jnp
from jax import lax
from jax.experimental import pallas as pl
from jax.experimental.pallas import tpu as pltpu
from jax.sharding import PartitionSpec as P

ORB = 12
PADDED = 16
PAIRS = ORB * ORB
LANES = 128
MESH = pl.DeviceIdType.MESH
F32 = jnp.float32
BF16 = jnp.bfloat16


def iota(shape, dim):
    return lax.broadcasted_iota(jnp.int32, shape, dim)


def turned(matrix, block):
    return lax.dot_general(matrix, block, (((1,), (1,)), ((), ())), preferred_element_type=F32)


def dot(left, right):
    return jnp.dot(left, right, preferred_element_type=F32)


def each(count, body):
    if count <= 2:
        for index in range(count):
            body(index)
    else:
        lax.fori_loop(0, count, lambda index, carry: (body(index), carry)[1], 0)


def kernel(
    slabs, energies, rows, atoms, edge, nbrs, freqs,
    green_far, sigma_far, neighbours_far, coupling_far, down_far, up_far, offsets_far, emit_far, absorb_far,
    total, refreshed,
    green, sigma_in, neighbours, coupling, send_down, send_up, offsets, w_emit, w_absorb, fetched,
    plain, across, source, product, lesser, partial, mixing, outgoing, halo, band,
    edge_send, edge_recv, halo_send, halo_recv,
):
    per = LANES // rows
    groups = atoms // per
    edges = outgoing.shape[1]
    fetches = [
        pltpu.make_async_copy(far, near, fetched.at[place])
        for place, (far, near) in enumerate((
            (green_far, green), (sigma_far, sigma_in), (down_far, send_down), (up_far, send_up),
            (neighbours_far, neighbours), (coupling_far, coupling),
            (offsets_far, offsets), (emit_far, w_emit), (absorb_far, w_absorb),
        ))
    ]
    for fetch in fetches:
        fetch.start()
    my_slab = lax.axis_index("slab")
    my_energy = lax.axis_index("energy")
    barrier = pltpu.get_barrier_semaphore()
    links = (
        (my_slab > 0, {"slab": my_slab - 1}),
        (my_slab < slabs - 1, {"slab": my_slab + 1}),
        (my_energy > 0, {"energy": my_energy - 1}),
        (my_energy < energies - 1, {"energy": my_energy + 1}),
    )
    for there, target in links:
        @pl.when(there)
        def _():
            pl.semaphore_signal(barrier, inc=1, device_id=target, device_id_type=MESH)

    for side in range(2):
        @pl.when(jnp.logical_not(links[side][0]))
        def _():
            for block in range(edges):
                lesser[groups + side * edges + block] = jnp.zeros((PAIRS, LANES), BF16)

        @pl.when(jnp.logical_not(links[2 + side][0]))
        def _():
            for block in range(groups):
                halo[1 + side, block] = jnp.zeros((PAIRS, LANES), BF16)

    spread = (ORB * PADDED, PAIRS)
    high, low = iota(spread, 0) // PADDED, iota(spread, 0) % PADDED
    real = low < ORB
    straight = jnp.where(real & (iota(spread, 1) == high * ORB + low), 1.0, 0.0).astype(BF16)
    swapped = jnp.where(real & (iota(spread, 1) == low * ORB + high), 1.0, 0.0).astype(BF16)
    square = (LANES, LANES)
    same_energy = iota(square, 0) % rows == iota(square, 1) % rows
    lane_atom = iota((1, LANES), 1) // rows

    fetches[0].wait()
    fetches[1].wait()

    def gathered(ref, group):
        pieces = [
            ref[:, (group * per + atom) * PAIRS:(group * per + atom + 1) * PAIRS]
            for atom in range(per)
        ]
        return jnp.concatenate(pieces, axis=0)

    for group in range(groups):
        stacked = gathered(green, group)
        plain[group] = turned(straight, stacked).reshape(ORB, PADDED, LANES)
        across[group] = turned(swapped, stacked).reshape(ORB, PADDED, LANES)
        source[group] = turned(straight, gathered(sigma_in, group)).reshape(ORB, PADDED, LANES)

    def sandwich(group):
        for row in range(ORB):
            left = plain[group, row, 0:1, :] * source[group, 0]
            for inner in range(1, ORB):
                left = left + plain[group, row, inner:inner + 1, :] * source[group, inner]
            right = left[0:1, :] * across[group, 0]
            for inner in range(1, ORB):
                right = right + left[inner:inner + 1, :] * across[group, inner]
            product[group, row * ORB:(row + 1) * ORB, :] = right[:ORB, :]
        return product[group].astype(BF16)

    def first(group):
        lesser[group] = sandwich(group)

    each(groups, first)
    for fetch in fetches[2:]:
        fetch.wait()

    def lane_values(values):
        result = jnp.full((1, LANES), values[0])
        for place in range(1, len(values)):
            result = jnp.where(lane_atom == place, values[place], result)
        return result

    def expand(pieces):
        full = jnp.concatenate([jnp.broadcast_to(piece, (rows, LANES)) for piece in pieces], axis=0)
        return jnp.where(same_energy, full, 0.0).astype(BF16)

    for side, sent in ((0, send_down), (1, send_up)):
        for block in range(edges):
            first_slot = block * per
            wanted = lane_values(
                [sent[0, first_slot + t] if first_slot + t < edge else jnp.int32(-1) for t in range(per)]
            )
            chosen = jnp.zeros((PAIRS, LANES), F32)
            for group in range(groups):
                pieces = [
                    jnp.where(wanted == group * per + atom, 1.0, 0.0) for atom in range(per)
                ]
                chosen = chosen + dot(lesser[group], expand(pieces))
            outgoing[side, block] = chosen.astype(BF16)

    count = sum(there.astype(jnp.int32) for there, _ in links)
    pl.semaphore_wait(barrier, count)

    def edge_copy(side, block):
        return pltpu.make_async_remote_copy(
            src_ref=outgoing.at[side, block],
            dst_ref=lesser.at[groups + (1 - side) * edges + block],
            send_sem=edge_send.at[side, block],
            recv_sem=edge_recv.at[1 - side, block],
            device_id=links[side][1],
            device_id_type=MESH,
        )

    def arriving_edge(side, block):
        return pltpu.make_async_remote_copy(
            src_ref=outgoing.at[side, block],
            dst_ref=lesser.at[groups + side * edges + block],
            send_sem=edge_send.at[side, block],
            recv_sem=edge_recv.at[side, block],
            device_id=links[side][1],
            device_id_type=MESH,
        )

    def halo_copy(side, group):
        return pltpu.make_async_remote_copy(
            src_ref=halo.at[0, group],
            dst_ref=halo.at[2 - side, group],
            send_sem=halo_send.at[side],
            recv_sem=halo_recv.at[1 - side, group],
            device_id=links[2 + side][1],
            device_id_type=MESH,
        )

    def halo_sent(side):
        return pltpu.make_async_remote_copy(
            src_ref=halo.at[0],
            dst_ref=halo.at[2 - side],
            send_sem=halo_send.at[side],
            recv_sem=halo_recv.at[1 - side, 0],
            device_id=links[2 + side][1],
            device_id_type=MESH,
        )

    def arriving_halo(side, group):
        return pltpu.make_async_remote_copy(
            src_ref=halo.at[0, group],
            dst_ref=halo.at[1 + side, group],
            send_sem=halo_send.at[side],
            recv_sem=halo_recv.at[side, group],
            device_id=links[2 + side][1],
            device_id_type=MESH,
        )

    for side in range(2):
        @pl.when(links[side][0])
        def _():
            for block in range(edges):
                edge_copy(side, block).start()

    slots = -(-(atoms + 2 * edge) // 8) * 8
    blocks = groups + 2 * edges
    wide = 2 if groups % 2 == 0 else 1
    units = groups // wide

    def weigh(unit):
        for inner in range(wide):
            group = unit * wide + inner
            lanes = slice(inner * LANES, (inner + 1) * LANES)
            slot = iota((slots, LANES), 0)
            weights = jnp.zeros((slots, LANES), F32)
            for column in range(nbrs):
                atom_of = lane_values([neighbours[group * per + t, column] for t in range(per)])
                strength = lane_values([coupling[group * per + t, column] for t in range(per)])
                weights = weights + jnp.where(slot == atom_of, strength, 0.0)
            coarse = weights.astype(BF16).astype(F32)
            for level, part in enumerate((coarse, weights - coarse)):
                for block in range(blocks):
                    side = (block - groups) // edges
                    pieces = []
                    for t in range(per):
                        number = block * per + t if block < groups else ((block - groups) % edges) * per + t
                        at = number if block < groups else atoms + side * edge + number
                        known = block < groups or number < edge
                        pieces.append(part[at:at + 1, :] if known else jnp.zeros((1, LANES), F32))
                    mixing[unit, level, block, :, lanes] = expand(pieces)

    each(units, weigh)

    def joined(unit, first, last):
        value = None
        for start in range(first, last, 2):
            stop = min(start + 2, last)
            left = jnp.concatenate([lesser[block] for block in range(start, stop)], axis=1)
            for level in range(2):
                right = mixing[unit, level, start:stop].reshape((stop - start) * LANES, wide * LANES)
                term = dot(left, right)
                value = term if value is None else value + term
        return value

    def mix_own(unit):
        partial[unit] = joined(unit, 0, groups)

    each(units, mix_own)

    for side in range(2):
        @pl.when(links[side][0])
        def _():
            for block in range(edges):
                arriving_edge(side, block).wait_recv()

    def mix_border(unit):
        value = (partial[unit] + joined(unit, groups, blocks)).astype(BF16)
        for inner in range(wide):
            group = unit * wide + inner
            halo[0, group] = value[:, inner * LANES:(inner + 1) * LANES]
            for side in range(2):
                @pl.when(links[2 + side][0])
                def _():
                    halo_copy(side, group).start()

    each(units, mix_border)

    tall = (rows, LANES)
    same_atom = iota(square, 0) // rows == iota(square, 1) // rows
    for place, shift in enumerate((0, rows, -rows)):
        distance = iota(tall, 1) % rows - iota(tall, 0) + shift
        weight = jnp.zeros(tall, F32)
        for freq in range(freqs):
            weight = jnp.where(distance == offsets[freq], w_emit[freq], weight)
            weight = jnp.where(distance == -offsets[freq], w_absorb[freq], weight)
        full = jnp.concatenate([weight] * per, axis=0)
        full = jnp.where(same_atom, full, 0.0).astype(BF16)
        for inner in range(wide):
            for other in range(wide):
                band[place, inner * LANES:(inner + 1) * LANES, other * LANES:(other + 1) * LANES] = (
                    full if inner == other else jnp.zeros(square, BF16)
                )

    def neighbour(place, unit):
        return [halo[place, unit * wide + inner] for inner in range(wide)]

    def band_own(unit):
        partial[unit] = dot(jnp.concatenate(neighbour(0, unit), axis=1), band[0])

    each(units, band_own)

    def finish(unit):
        for inner in range(wide):
            group = unit * wide + inner
            for side in range(2):
                @pl.when(links[2 + side][0])
                def _():
                    arriving_halo(side, group).wait_recv()
            both = jnp.concatenate([halo[1, group], halo[2, group]], axis=1)
            sides = band[1:3, 0:LANES, 0:LANES].reshape(2 * LANES, LANES)
            value = partial[unit, :, inner * LANES:(inner + 1) * LANES] + dot(both, sides)
            total[group] = value.astype(BF16)
            product[group] = total[group].astype(F32)
            for row in range(ORB):
                source[group, row, 0:ORB, :] = (
                    source[group, row, 0:ORB, :] + product[group, row * ORB:(row + 1) * ORB, :]
                )
            refreshed[group] = sandwich(group)

    each(units, finish)

    for side in range(2):
        @pl.when(links[side][0])
        def _():
            for block in range(edges):
                edge_copy(side, block).wait_send()

        @pl.when(links[2 + side][0])
        def _():
            halo_sent(side).wait_send()


def finishing(rows, total, refreshed, sigma_out, g_out, sigma_near, g_near, written):
    per = LANES // rows
    square = (LANES, LANES)
    identity = jnp.where(iota(square, 0) == iota(square, 1), 1.0, 0.0).astype(BF16)
    copies = []
    for place, (values, near, out) in enumerate(((total, sigma_near, sigma_out), (refreshed, g_near, g_out))):
        for group in range(total.shape[0]):
            back = turned(identity, values[group]).astype(BF16)
            for atom in range(per):
                at = (group * per + atom) * PAIRS
                near[:, at:at + PAIRS] = back[atom * rows:(atom + 1) * rows, :]
        copies.append(pltpu.make_async_copy(near, out, written.at[place]))
        copies[-1].start()
    for copy in copies:
        copy.wait()


def on_device(slabs, energies, green, sigma_in, neighbours, coupling, send_down, send_up, offsets, w_emit, w_absorb):
    rows, flat = green.shape
    atoms = flat // PAIRS
    edge = send_down.shape[1]
    per = LANES // rows
    groups = atoms // per
    edges = -(-edge // per)
    wide = 2 if groups % 2 == 0 else 1
    smalls = (neighbours, coupling, send_down, send_up, offsets, w_emit, w_absorb)
    vmem = pl.BlockSpec(memory_space=pltpu.VMEM)
    far = pl.BlockSpec(memory_space=pltpu.HBM)
    body = functools.partial(
        kernel, slabs, energies, rows, atoms, edge, neighbours.shape[1], offsets.shape[0]
    )
    shape = jax.ShapeDtypeStruct((rows, flat), BF16)
    turned_shape = pltpu.VMEM((groups, PAIRS, LANES), BF16)
    total, refreshed = pl.pallas_call(
        body,
        out_shape=(turned_shape, turned_shape),
        in_specs=[far] * 9,
        out_specs=(vmem, vmem),
        scratch_shapes=[
            pltpu.VMEM(green.shape, BF16),
            pltpu.VMEM(green.shape, BF16),
            *[pltpu.SMEM(small.shape, small.dtype) for small in smalls],
            pltpu.SemaphoreType.DMA((9,)),
            pltpu.VMEM((groups, ORB, PADDED, LANES), F32),
            pltpu.VMEM((groups, ORB, PADDED, LANES), F32),
            pltpu.VMEM((groups, ORB, PADDED, LANES), F32),
            pltpu.VMEM((groups, PAIRS, LANES), F32),
            pltpu.VMEM((groups + 2 * edges, PAIRS, LANES), BF16),
            pltpu.VMEM((groups // wide, PAIRS, wide * LANES), F32),
            pltpu.VMEM((groups // wide, 2, groups + 2 * edges, LANES, wide * LANES), BF16),
            pltpu.VMEM((2, edges, PAIRS, LANES), BF16),
            pltpu.VMEM((3, groups, PAIRS, LANES), BF16),
            pltpu.VMEM((3, wide * LANES, wide * LANES), BF16),
            pltpu.SemaphoreType.DMA((2, edges)),
            pltpu.SemaphoreType.DMA((2, edges)),
            pltpu.SemaphoreType.DMA((2,)),
            pltpu.SemaphoreType.DMA((2, groups)),
        ],
        compiler_params=pltpu.CompilerParams(
            collective_id=0, has_side_effects=True
        ),
    )(green, sigma_in, *smalls)
    return pl.pallas_call(
        functools.partial(finishing, rows),
        out_shape=(shape, shape),
        in_specs=[vmem] * 2,
        out_specs=(far, far),
        scratch_shapes=[
            pltpu.VMEM((rows, flat), BF16),
            pltpu.VMEM((rows, flat), BF16),
            pltpu.SemaphoreType.DMA((2,)),
        ],
        compiler_params=pltpu.CompilerParams(vmem_limit_bytes=(4 + groups) << 20),
    )(total, refreshed)


def solution(mesh):
    placed = (
        P("energy", "slab"),
        P("energy", "slab"),
        P("slab", None),
        P("slab", None),
        P("slab", None),
        P("slab", None),
        P(),
        P(),
        P(),
    )
    return jax.shard_map(
        functools.partial(on_device, mesh.shape["slab"], mesh.shape["energy"]),
        mesh=mesh,
        in_specs=placed,
        out_specs=(P("energy", "slab"), P("energy", "slab")),
        check_vma=False,
    )
```

profile of v0, /device:TPU:1, one launch (start us, length us, event | category | flops | bytes accessed | tf_op | source)
XLA Modules:
  0.0 11.8 jit_solution(6208982017906187122)
XLA Ops:
  0.6 10.2 %shard_map.104 = (bf16[2,144,128]{2,1,0:T(8,128)(2,1)S(1)}, bf16[2,144,128]{2,1,0:T(8,128)(2,1)S(1)}) custom-call(bf16[32,1152]{1,0:T(8,128)(2,1)} %green_far.1, bf16[32,1152]{1,0:T(8,128)(2,1)} %sigma_far.1, s32[8,8]{1,0:T(8,128)} %neighbours_far.1, f32[8,8]{1,0:T(8,128)} %coupling_far.1, s32[1,2]{1,0:T(1,128)} %down_far.1, s32[1,2]{1,0:T(1,128)} %up_far.1, ...), custom_call_target="tpu_custom_call" | custom-call | tf_op jit(solution)/shard_map/pallas_call | solution.py:362
  10.8 1.0 %shard_map.105 = (bf16[32,1152]{1,0:T(8,128)(2,1)}, bf16[32,1152]{1,0:T(8,128)(2,1)}) custom-call(bf16[2,144,128]{2,1,0:T(8,128)(2,1)S(1)} %get-tuple-element.4.total, bf16[2,144,128]{2,1,0:T(8,128)(2,1)S(1)} %get-tuple-element.5.refreshed), custom_call_target="tpu_custom_call" | custom-call | tf_op jit(solution)/shard_map/pallas_call | solution.py:391
where the time goes:
time: 12 us; the launch traced here: 11.8 us
  Pallas kernels  11.2 us (93%)
  between operations  0.64 us (5%)
    pallas_call x1, Pallas kernels, on_device(): pl.pallas_call(body, out_shape=(turned_shape, turned_shape), in_specs=[fa...  10.2 us
    pallas_call x1, Pallas kernels, on_device(): pl.pallas_call(functools.partial(finishing, rows), out_shape=(shape, shap...  0.97 us

commit v1 on v0

--- a/solution.py
+++ b/solution.py
@@ -343,6 +343,358 @@
         copy.wait()
 
 
+def compact(
+    slabs, energies, rows, atoms, edge, nbrs, freqs,
+    green_far, sigma_far, neighbours_far, coupling_far, down_far, up_far, offsets_far, emit_far, absorb_far,
+    sigma_near, g_near,
+    green, sigma_in, neighbours, coupling, send_down, send_up, offsets, w_emit, w_absorb, fetched,
+    cut, across, source, product, lesser, partial, mixing, border, outgoing, arrived, halo, own_band, far_band,
+    edge_send, edge_recv, halo_send, halo_recv, relay_send,
+):
+    per = LANES // rows
+    groups = atoms // per
+    last = groups - 1
+    half = PAIRS // 2
+    middle = LANES // 2
+    span = groups * LANES
+    fetches = [
+        pltpu.make_async_copy(far, near, fetched.at[place])
+        for place, (far, near) in enumerate((
+            (green_far, green), (sigma_far, sigma_in), (down_far, send_down), (up_far, send_up),
+            (neighbours_far, neighbours), (coupling_far, coupling),
+            (offsets_far, offsets), (emit_far, w_emit), (absorb_far, w_absorb),
+        ))
+    ]
+    for fetch in fetches:
+        fetch.start()
+    my_slab = lax.axis_index("slab")
+    my_energy = lax.axis_index("energy")
+    ahead = 1 - 2 * (my_energy % 2)
+    relayed = my_slab == slabs - 1
+    beyond = my_energy - ahead
+    inside = (beyond >= 0) & (beyond < energies)
+    onward, origin = my_energy + 2 * ahead, my_energy - 2 * ahead
+    relays = relayed & (onward >= 0) & (onward < energies)
+    barrier = pltpu.get_barrier_semaphore()
+    links = (
+        (my_slab > 0, {"slab": my_slab - 1}),
+        (my_slab < slabs - 1, {"slab": my_slab + 1}),
+        (my_energy >= 0, {"energy": my_energy + ahead}),
+        (inside, {"energy": beyond}),
+        (relays, {"energy": onward}),
+        (relayed & inside, {"energy": origin}),
+    )
+    for there, target in links:
+        @pl.when(there)
+        def _():
+            pl.semaphore_signal(barrier, inc=1, device_id=target, device_id_type=MESH)
+
+    for side in range(2):
+        @pl.when(jnp.logical_not(links[side][0]))
+        def _():
+            arrived[side] = jnp.zeros((half, LANES), BF16)
+
+    @pl.when(jnp.logical_not(inside))
+    def _():
+        for group in range(groups):
+            halo[2, group] = jnp.zeros((PAIRS, LANES), BF16)
+
+    spread = (ORB * PADDED, PAIRS)
+    high, low = iota(spread, 0) // PADDED, iota(spread, 0) % PADDED
+    swapped = jnp.where((low < ORB) & (iota(spread, 1) == low * ORB + high), 1.0, 0.0).astype(BF16)
+    compacted = (PAIRS, PAIRS)
+    straight = jnp.where(iota(compacted, 0) == iota(compacted, 1), 1.0, 0.0).astype(BF16)
+    square = (LANES, LANES)
+
+    def load(slot, blocks):
+        stacked = jnp.concatenate([cut[0, block] for block in blocks], axis=0)
+        across[slot] = turned(swapped, stacked).reshape(ORB, PADDED, LANES)
+        stacked = jnp.concatenate([cut[1, block] for block in blocks], axis=0)
+        source[slot] = turned(straight, stacked)
+
+    def sandwich(slot):
+        columns = []
+        for column in range(ORB):
+            left = across[slot, 0] * source[slot, column:column + 1, :]
+            for inner in range(1, ORB):
+                at = inner * ORB + column
+                left = left + across[slot, inner] * source[slot, at:at + 1, :]
+            columns.append(left)
+        for column in range(ORB):
+            right = columns[0] * across[slot, 0, column:column + 1, :]
+            for inner in range(1, ORB):
+                right = right + columns[inner] * across[slot, inner, column:column + 1, :]
+            product[slot, pl.ds(column, ORB, stride=ORB), :] = right[:ORB, :]
+        return product[slot]
+
+    for fetch in fetches[:4]:
+        fetch.wait()
+    for place, ref in enumerate((green, sigma_in)):
+        for atom in range(atoms):
+            cut[place, atom] = ref[:, atom * PAIRS:(atom + 1) * PAIRS]
+
+    load(groups, [send_down[0, t] for t in range(edge)] + [send_up[0, t] for t in range(edge)])
+    edges = sandwich(groups)
+    top, bottom = edges[:half], edges[half:]
+    lower = iota((half, LANES), 1) < middle
+    outgoing[0] = jnp.where(lower, top, pltpu.roll(bottom, middle, 1)).astype(BF16)
+    outgoing[1] = jnp.where(lower, pltpu.roll(top, middle, 1), bottom).astype(BF16)
+
+    count = sum(there.astype(jnp.int32) for there, _ in links)
+    pl.semaphore_wait(barrier, count)
+
+    def edge_copy(side, slot):
+        return pltpu.make_async_remote_copy(
+            src_ref=outgoing.at[side],
+            dst_ref=arrived.at[slot],
+            send_sem=edge_send.at[side],
+            recv_sem=edge_recv.at[slot],
+            device_id=links[side][1],
+            device_id_type=MESH,
+        )
+
+    def halo_copy(kind, group):
+        return pltpu.make_async_remote_copy(
+            src_ref=halo.at[0, group],
+            dst_ref=halo.at[1 + kind, group],
+            send_sem=halo_send.at[kind, group],
+            recv_sem=halo_recv.at[kind, group],
+            device_id=links[2 + kind][1],
+            device_id_type=MESH,
+        )
+
+    def relay_copy():
+        return pltpu.make_async_remote_copy(
+            src_ref=halo.at[1, last],
+            dst_ref=halo.at[2, last],
+            send_sem=relay_send,
+            recv_sem=halo_recv.at[1, last],
+            device_id=links[4][1],
+            device_id_type=MESH,
+        )
+
+    for side in range(2):
+        @pl.when(links[side][0])
+        def _():
+            edge_copy(side, 1 - side).start()
+
+    for group in range(groups):
+        load(group, range(group * per, (group + 1) * per))
+    for group in range(groups):
+        lesser[:, group * LANES:(group + 1) * LANES] = sandwich(group).astype(BF16)
+
+    for fetch in fetches[4:]:
+        fetch.wait()
+    slots = -(-(atoms + 2 * edge) // 8) * 8
+    lane_atom = iota((1, span), 1) // rows
+
+    def lane_values(values):
+        result = jnp.full((1, span), values[0])
+        for place in range(1, len(values)):
+            result = jnp.where(lane_atom == place, values[place], result)
+        return result
+
+    slot_of = iota((slots, span), 0)
+    weights = jnp.zeros((slots, span), F32)
+    for column in range(nbrs):
+        atom_of = lane_values([neighbours[atom, column] for atom in range(atoms)])
+        strength = lane_values([coupling[atom, column] for atom in range(atoms)])
+        weights = weights + jnp.where(slot_of == atom_of, strength, 0.0)
+    tall = (rows, span)
+    same_energy = iota(tall, 0) == iota(tall, 1) % rows
+
+    def expanded(at):
+        return jnp.where(same_energy, jnp.broadcast_to(weights[at:at + 1, :], tall), 0.0).astype(BF16)
+
+    for atom in range(atoms):
+        mixing[atom * rows:(atom + 1) * rows, :] = expanded(atom)
+    empty = jnp.zeros((middle, span), BF16)
+    for side in range(2):
+        start = side * LANES
+        for t in range(edge):
+            part = expanded(atoms + side * edge + t)
+            border[start + t * rows:start + (t + 1) * rows, 0:span] = part
+            border[start + middle + t * rows:start + middle + (t + 1) * rows, span:2 * span] = part
+        border[start:start + middle, span:2 * span] = empty
+        border[start + middle:start + LANES, 0:span] = empty
+
+    partial[...] = dot(lesser[...], mixing[...])
+
+    for side in range(2):
+        @pl.when(links[side][0])
+        def _():
+            edge_copy(side, side).wait_recv()
+
+    crossing = dot(jnp.concatenate([arrived[0], arrived[1]], axis=1), border[...])
+    crossing = jnp.concatenate([crossing[:, 0:span], crossing[:, span:2 * span]], axis=0)
+    mixed = (partial[...] + crossing).astype(BF16)
+    for group in range(groups):
+        halo[0, group] = mixed[:, group * LANES:(group + 1) * LANES]
+
+    direct = jnp.logical_not(relayed)
+
+    @pl.when(relayed)
+    def _():
+        halo_copy(0, last).start()
+
+    for group in range(groups):
+        @pl.when(inside if group < last else inside & direct)
+        def _():
+            halo_copy(1, group).start()
+
+        if group < last:
+            halo_copy(0, group).start()
+
+    @pl.when(direct)
+    def _():
+        halo_copy(0, last).start()
+
+    same_atom = iota(square, 0) // rows == iota(square, 1) // rows
+    narrow = (rows, LANES)
+    distance = iota(narrow, 1) % rows - iota(narrow, 0)
+    near_weight = jnp.zeros(narrow, F32)
+    ahead_weight = jnp.zeros(narrow, F32)
+    behind_weight = jnp.zeros(narrow, F32)
+    ahead_gap = rows - ahead * distance
+    behind_gap = rows + ahead * distance
+    upward = ahead > 0
+    for freq in range(freqs):
+        offset, emit, absorb = offsets[freq], w_emit[freq], w_absorb[freq]
+        near_weight = jnp.where(distance == offset, emit, near_weight)
+        near_weight = jnp.where(distance == -offset, absorb, near_weight)
+        ahead_weight = jnp.where(ahead_gap == offset, jnp.where(upward, absorb, emit), ahead_weight)
+        behind_weight = jnp.where(behind_gap == offset, jnp.where(upward, emit, absorb), behind_weight)
+
+    def band(weight):
+        return jnp.where(same_atom, jnp.concatenate([weight] * per, axis=0), 0.0).astype(BF16)
+
+    own_band[...] = band(near_weight)
+    far_band[0:LANES, :] = band(ahead_weight)
+    far_band[LANES:2 * LANES, :] = band(behind_weight)
+    for group in range(groups):
+        partial[:, group * LANES:(group + 1) * LANES] = dot(halo[0, group], own_band[...])
+
+    @pl.when(relayed)
+    def _():
+        halo_copy(0, last).wait_recv()
+
+    @pl.when(relays)
+    def _():
+        relay_copy().start()
+
+    identity = jnp.where(iota(square, 0) == iota(square, 1), 1.0, 0.0).astype(BF16)
+
+    def place_rows(near, group, values):
+        back = turned(identity, values).astype(BF16)
+        for atom in range(per):
+            at = (group * per + atom) * PAIRS
+            near[:, at:at + PAIRS] = back[atom * rows:(atom + 1) * rows, :]
+
+    for group in range(groups):
+        if group < last:
+            halo_copy(0, group).wait_recv()
+        else:
+            @pl.when(direct)
+            def _():
+                halo_copy(0, last).wait_recv()
+
+        @pl.when(inside)
+        def _():
+            halo_copy(1, group).wait_recv()
+
+        both = jnp.concatenate([halo[1, group], halo[2, group]], axis=1)
+        value = partial[:, group * LANES:(group + 1) * LANES] + dot(both, far_band[...])
+        total = value.astype(BF16)
+        place_rows(sigma_near, group, total)
+        source[group] = source[group] + total.astype(F32)
+        place_rows(g_near, group, sandwich(group).astype(BF16))
+
+    for side in range(2):
+        @pl.when(links[side][0])
+        def _():
+            edge_copy(side, 1 - side).wait_send()
+
+    for group in range(groups):
+        halo_copy(0, group).wait_send()
+
+        @pl.when(inside if group < last else inside & direct)
+        def _():
+            halo_copy(1, group).wait_send()
+
+    @pl.when(relays)
+    def _():
+        relay_copy().wait_send()
+
+
+def delivering(sigma_near, g_near, sigma_out, g_out, written):
+    copies = [
+        pltpu.make_async_copy(near, out, written.at[place])
+        for place, (near, out) in enumerate(((sigma_near, sigma_out), (g_near, g_out)))
+    ]
+    for copy in copies:
+        copy.start()
+    for copy in copies:
+        copy.wait()
+
+
+def on_device_compact(slabs, energies, green, sigma_in, *smalls):
+    rows, flat = green.shape
+    atoms = flat // PAIRS
+    neighbours, _, send_down, _, offsets, _, _ = smalls
+    edge = send_down.shape[1]
+    per = LANES // rows
+    groups = atoms // per
+    span = groups * LANES
+    vmem = pl.BlockSpec(memory_space=pltpu.VMEM)
+    far = pl.BlockSpec(memory_space=pltpu.HBM)
+    body = functools.partial(
+        compact, slabs, energies, rows, atoms, edge, neighbours.shape[1], offsets.shape[0]
+    )
+    shape = jax.ShapeDtypeStruct((rows, flat), BF16)
+    near_shape = pltpu.VMEM((rows, flat), BF16)
+    near = pl.pallas_call(
+        body,
+        out_shape=(near_shape, near_shape),
+        in_specs=[far] * 9,
+        out_specs=(vmem, vmem),
+        scratch_shapes=[
+            pltpu.VMEM(green.shape, BF16),
+            pltpu.VMEM(green.shape, BF16),
+            *[pltpu.SMEM(small.shape, small.dtype) for small in smalls],
+            pltpu.SemaphoreType.DMA((9,)),
+            pltpu.VMEM((2, atoms, rows, PAIRS), BF16),
+            pltpu.VMEM((groups + 1, ORB, PADDED, LANES), F32),
+            pltpu.VMEM((groups + 1, PAIRS, LANES), F32),
+            pltpu.VMEM((groups + 1, PAIRS, LANES), F32),
+            pltpu.VMEM((PAIRS, span), BF16),
+            pltpu.VMEM((PAIRS, span), F32),
+            pltpu.VMEM((span, span), BF16),
+            pltpu.VMEM((2 * LANES, 2 * span), BF16),
+            pltpu.VMEM((2, PAIRS // 2, LANES), BF16),
+            pltpu.VMEM((2, PAIRS // 2, LANES), BF16),
+            pltpu.VMEM((3, groups, PAIRS, LANES), BF16),
+            pltpu.VMEM((LANES, LANES), BF16),
+            pltpu.VMEM((2 * LANES, LANES), BF16),
+            pltpu.SemaphoreType.DMA((2,)),
+            pltpu.SemaphoreType.DMA((2,)),
+            pltpu.SemaphoreType.DMA((2, groups)),
+            pltpu.SemaphoreType.DMA((2, groups)),
+            pltpu.SemaphoreType.DMA,
+        ],
+        compiler_params=pltpu.CompilerParams(
+            collective_id=0, has_side_effects=True
+        ),
+    )(green, sigma_in, *smalls)
+    return pl.pallas_call(
+        delivering,
+        out_shape=(shape, shape),
+        in_specs=[vmem] * 2,
+        out_specs=(far, far),
+        scratch_shapes=[pltpu.SemaphoreType.DMA((2,))],
+        compiler_params=pltpu.CompilerParams(vmem_limit_bytes=(4 + groups) << 20),
+    )(*near)
+
+
 def on_device(slabs, energies, green, sigma_in, neighbours, coupling, send_down, send_up, offsets, w_emit, w_absorb):
     rows, flat = green.shape
     atoms = flat // PAIRS
@@ -352,6 +704,8 @@
     edges = -(-edge // per)
     wide = 2 if groups % 2 == 0 else 1
     smalls = (neighbours, coupling, send_down, send_up, offsets, w_emit, w_absorb)
+    if 2 * edge == per and groups == 2 and energies % 2 == 0:
+        return on_device_compact(slabs, energies, green, sigma_in, *smalls)
     vmem = pl.BlockSpec(memory_space=pltpu.VMEM)
     far = pl.BlockSpec(memory_space=pltpu.HBM)
     body = functools.partial(

time: 12 us -> 11.5 us (0.958)
  Pallas kernels: 11.2 us -> 10.7 us
    pallas_call x2, Pallas kernels: 11.2 us -> 10.7 us  [the longest x1 10 us: on_device_compact(): pl.pallas_call(body, out_shape=(near_shape, near_shape), in_specs=[far] *...]
where the time goes in v1:
time: 11.5 us; the launch traced here: 11.3 us
  Pallas kernels  10.7 us (93%)
  between operations  0.64 us (6%)
    pallas_call x1, Pallas kernels, on_device_compact(): pl.pallas_call(body, out_shape=(near_shape, near_shape), in_specs=[far] *...  10 us
    pallas_call x1, Pallas kernels, on_device_compact(): pl.pallas_call(delivering, out_shape=(shape, shape), in_specs=[vmem] * 2,...  0.68 us

profile of v1, /device:TPU:1, one launch (start us, length us, event | category | flops | bytes accessed | tf_op | source)
XLA Modules:
  0.0 11.3 jit_solution(1355842018310227640)
XLA Ops:
  0.6 10.0 %shard_map.104 = (bf16[32,1152]{1,0:T(8,128)(2,1)S(1)}, bf16[32,1152]{1,0:T(8,128)(2,1)S(1)}) custom-call(bf16[32,1152]{1,0:T(8,128)(2,1)} %green_far.1, bf16[32,1152]{1,0:T(8,128)(2,1)} %sigma_far.1, s32[8,8]{1,0:T(8,128)} %neighbours_far.1, f32[8,8]{1,0:T(8,128)} %coupling_far.1, s32[1,2]{1,0:T(1,128)} %down_far.1, s32[1,2]{1,0:T(1,128)} %up_far.1, ...), custom_call_target="tpu_custom_call" | custom-call | tf_op jit(solution)/shard_map/pallas_call | solution.py:655
  10.7 0.7 %shard_map.105 = (bf16[32,1152]{1,0:T(8,128)(2,1)}, bf16[32,1152]{1,0:T(8,128)(2,1)}) custom-call(bf16[32,1152]{1,0:T(8,128)(2,1)S(1)} %get-tuple-element.4.sigma_near, bf16[32,1152]{1,0:T(8,128)(2,1)S(1)} %get-tuple-element.5.g_near), custom_call_target="tpu_custom_call" | custom-call | tf_op jit(solution)/shard_map/pallas_call | solution.py:688

commit v2 on v1

--- a/solution.py
+++ b/solution.py
@@ -348,8 +348,8 @@
     green_far, sigma_far, neighbours_far, coupling_far, down_far, up_far, offsets_far, emit_far, absorb_far,
     sigma_near, g_near,
     green, sigma_in, neighbours, coupling, send_down, send_up, offsets, w_emit, w_absorb, fetched,
-    cut, across, source, product, lesser, partial, mixing, border, outgoing, arrived, halo, own_band, far_band,
-    edge_send, edge_recv, halo_send, halo_recv, relay_send,
+    cut, across, source, product, lesser, partial, mixing, border, outgoing, arrived, crossed, halo, own_band, far_band,
+    edge_send, edge_recv, cross_send, cross_recv, halo_send, halo_recv, relay_send,
 ):
     per = LANES // rows
     groups = atoms // per
@@ -370,6 +370,10 @@
     my_slab = lax.axis_index("slab")
     my_energy = lax.axis_index("energy")
     ahead = 1 - 2 * (my_energy % 2)
+    odd = my_slab % 2 == 1
+    below, above = my_slab > 0, my_slab < slabs - 1
+    receives = odd & above
+    crosses = jnp.logical_not(odd) & below
     relayed = my_slab == slabs - 1
     beyond = my_energy - ahead
     inside = (beyond >= 0) & (beyond < energies)
@@ -377,22 +381,31 @@
     relays = relayed & (onward >= 0) & (onward < energies)
     barrier = pltpu.get_barrier_semaphore()
     links = (
-        (my_slab > 0, {"slab": my_slab - 1}),
-        (my_slab < slabs - 1, {"slab": my_slab + 1}),
+        (below, {"slab": my_slab - 1}),
+        (above, {"slab": my_slab + 1}),
         (my_energy >= 0, {"energy": my_energy + ahead}),
         (inside, {"energy": beyond}),
-        (relays, {"energy": onward}),
+    )
+    greeted = links + (
         (relayed & inside, {"energy": origin}),
+        (receives, {"energy": my_energy + ahead, "slab": my_slab + 1}),
+        (receives & inside, {"energy": beyond, "slab": my_slab + 1}),
     )
-    for there, target in links:
+    awaited = [there for there, _ in links] + [relays, crosses, crosses & inside]
+    for there, target in greeted:
         @pl.when(there)
         def _():
             pl.semaphore_signal(barrier, inc=1, device_id=target, device_id_type=MESH)
 
+    early = (below, above & jnp.logical_not(odd))
     for side in range(2):
-        @pl.when(jnp.logical_not(links[side][0]))
+        @pl.when(jnp.logical_not(early[side]))
         def _():
             arrived[side] = jnp.zeros((half, LANES), BF16)
+
+    @pl.when(receives & jnp.logical_not(inside))
+    def _():
+        crossed[2] = jnp.zeros((half, LANES), BF16)
 
     @pl.when(jnp.logical_not(inside))
     def _():
@@ -440,7 +453,7 @@
     outgoing[0] = jnp.where(lower, top, pltpu.roll(bottom, middle, 1)).astype(BF16)
     outgoing[1] = jnp.where(lower, pltpu.roll(top, middle, 1), bottom).astype(BF16)
 
-    count = sum(there.astype(jnp.int32) for there, _ in links)
+    count = sum(there.astype(jnp.int32) for there in awaited)
     pl.semaphore_wait(barrier, count)
 
     def edge_copy(side, slot):
@@ -453,6 +466,17 @@
             device_id_type=MESH,
         )
 
+    def cross_copy(kind):
+        energy = (my_energy, my_energy + ahead, beyond)[kind]
+        return pltpu.make_async_remote_copy(
+            src_ref=outgoing.at[0],
+            dst_ref=crossed.at[kind],
+            send_sem=cross_send.at[kind],
+            recv_sem=cross_recv.at[kind],
+            device_id={"energy": energy, "slab": my_slab - 1},
+            device_id_type=MESH,
+        )
+
     def halo_copy(kind, group):
         return pltpu.make_async_remote_copy(
             src_ref=halo.at[0, group],
@@ -469,14 +493,20 @@
             dst_ref=halo.at[2, last],
             send_sem=relay_send,
             recv_sem=halo_recv.at[1, last],
-            device_id=links[4][1],
+            device_id={"energy": onward},
             device_id_type=MESH,
         )
 
+    sends = (odd, above)
     for side in range(2):
-        @pl.when(links[side][0])
+        @pl.when(sends[side])
         def _():
             edge_copy(side, 1 - side).start()
+
+    for kind in range(3):
+        @pl.when(crosses if kind < 2 else crosses & inside)
+        def _():
+            cross_copy(kind).start()
 
     for group in range(groups):
         load(group, range(group * per, (group + 1) * per))
@@ -521,13 +551,15 @@
     partial[...] = dot(lesser[...], mixing[...])
 
     for side in range(2):
-        @pl.when(links[side][0])
+        @pl.when(early[side])
         def _():
             edge_copy(side, side).wait_recv()
 
+    def unfolded(values):
+        return jnp.concatenate([values[:, 0:span], values[:, span:2 * span]], axis=0)
+
     crossing = dot(jnp.concatenate([arrived[0], arrived[1]], axis=1), border[...])
-    crossing = jnp.concatenate([crossing[:, 0:span], crossing[:, span:2 * span]], axis=0)
-    mixed = (partial[...] + crossing).astype(BF16)
+    mixed = (partial[...] + unfolded(crossing)).astype(BF16)
     for group in range(groups):
         halo[0, group] = mixed[:, group * LANES:(group + 1) * LANES]
 
@@ -582,6 +614,22 @@
     def _():
         relay_copy().start()
 
+    @pl.when(receives)
+    def _():
+        pieces = []
+        for kind in range(3):
+            if kind < 2:
+                cross_copy(kind).wait_recv()
+            else:
+                @pl.when(inside)
+                def _():
+                    cross_copy(kind).wait_recv()
+            pieces.append(unfolded(dot(crossed[kind], border[LANES:2 * LANES, :])).astype(BF16))
+        for group in range(groups):
+            lanes = slice(group * LANES, (group + 1) * LANES)
+            far = jnp.concatenate([pieces[1][:, lanes], pieces[2][:, lanes]], axis=1)
+            partial[:, lanes] = partial[:, lanes] + dot(pieces[0][:, lanes], own_band[...]) + dot(far, far_band[...])
+
     identity = jnp.where(iota(square, 0) == iota(square, 1), 1.0, 0.0).astype(BF16)
 
     def place_rows(near, group, values):
@@ -610,9 +658,14 @@
         place_rows(g_near, group, sandwich(group).astype(BF16))
 
     for side in range(2):
-        @pl.when(links[side][0])
+        @pl.when(sends[side])
         def _():
             edge_copy(side, 1 - side).wait_send()
+
+    for kind in range(3):
+        @pl.when(crosses if kind < 2 else crosses & inside)
+        def _():
+            cross_copy(kind).wait_send()
 
     for group in range(groups):
         halo_copy(0, group).wait_send()
@@ -672,11 +725,14 @@
             pltpu.VMEM((2 * LANES, 2 * span), BF16),
             pltpu.VMEM((2, PAIRS // 2, LANES), BF16),
             pltpu.VMEM((2, PAIRS // 2, LANES), BF16),
+            pltpu.VMEM((3, PAIRS // 2, LANES), BF16),
             pltpu.VMEM((3, groups, PAIRS, LANES), BF16),
             pltpu.VMEM((LANES, LANES), BF16),
             pltpu.VMEM((2 * LANES, LANES), BF16),
             pltpu.SemaphoreType.DMA((2,)),
             pltpu.SemaphoreType.DMA((2,)),
+            pltpu.SemaphoreType.DMA((3,)),
+            pltpu.SemaphoreType.DMA((3,)),
             pltpu.SemaphoreType.DMA((2, groups)),
             pltpu.SemaphoreType.DMA((2, groups)),
             pltpu.SemaphoreType.DMA,

time: 11.5 us -> 10.9 us (0.948)
  the two profiles are of different devices: /device:TPU:1 before, /device:TPU:9 now
where the time goes in v2:
time: 10.9 us; the launch traced here: 10.8 us
  Pallas kernels  10.1 us (93%)
  between operations  0.64 us (6%)
    pallas_call x1, Pallas kernels, on_device_compact(): pl.pallas_call(body, out_shape=(near_shape, near_shape), in_specs=[far] *...  9.45 us
    pallas_call x1, Pallas kernels, on_device_compact(): pl.pallas_call(delivering, out_shape=(shape, shape), in_specs=[vmem] * 2,...  0.68 us

profile of v2, /device:TPU:9, one launch (start us, length us, event | category | flops | bytes accessed | tf_op | source)
XLA Modules:
  0.0 10.8 jit_solution(11634159913930636355)
XLA Ops:
  0.6 9.4 %shard_map.104 = (bf16[32,1152]{1,0:T(8,128)(2,1)S(1)}, bf16[32,1152]{1,0:T(8,128)(2,1)S(1)}) custom-call(bf16[32,1152]{1,0:T(8,128)(2,1)} %green_far.1, bf16[32,1152]{1,0:T(8,128)(2,1)} %sigma_far.1, s32[8,8]{1,0:T(8,128)} %neighbours_far.1, f32[8,8]{1,0:T(8,128)} %coupling_far.1, s32[1,2]{1,0:T(1,128)} %down_far.1, s32[1,2]{1,0:T(1,128)} %up_far.1, ...), custom_call_target="tpu_custom_call" | custom-call | tf_op jit(solution)/shard_map/pallas_call | solution.py:708
  10.1 0.7 %shard_map.105 = (bf16[32,1152]{1,0:T(8,128)(2,1)}, bf16[32,1152]{1,0:T(8,128)(2,1)}) custom-call(bf16[32,1152]{1,0:T(8,128)(2,1)S(1)} %get-tuple-element.4.sigma_near, bf16[32,1152]{1,0:T(8,128)(2,1)S(1)} %get-tuple-element.5.g_near), custom_call_target="tpu_custom_call" | custom-call | tf_op jit(solution)/shard_map/pallas_call | solution.py:744

commit v3 on v1

--- a/solution.py
+++ b/solution.py
@@ -370,6 +370,9 @@
     my_slab = lax.axis_index("slab")
     my_energy = lax.axis_index("energy")
     ahead = 1 - 2 * (my_energy % 2)
+    odd = my_slab % 2 == 1
+    even = jnp.logical_not(odd)
+    exists = (my_slab > 0, my_slab < slabs - 1)
     relayed = my_slab == slabs - 1
     beyond = my_energy - ahead
     inside = (beyond >= 0) & (beyond < energies)
@@ -377,25 +380,33 @@
     relays = relayed & (onward >= 0) & (onward < energies)
     barrier = pltpu.get_barrier_semaphore()
     links = (
-        (my_slab > 0, {"slab": my_slab - 1}),
-        (my_slab < slabs - 1, {"slab": my_slab + 1}),
+        (exists[0], {"slab": my_slab - 1}),
+        (exists[1], {"slab": my_slab + 1}),
         (my_energy >= 0, {"energy": my_energy + ahead}),
         (inside, {"energy": beyond}),
-        (relays, {"energy": onward}),
-        (relayed & inside, {"energy": origin}),
     )
-    for there, target in links:
+    greeted = list(links) + [(relayed & inside, {"energy": origin})]
+    awaited = [there for there, _ in links] + [relays]
+    for side in range(2):
+        for energy, there in ((my_energy + ahead, exists[side]), (beyond, exists[side] & inside)):
+            greeted.append((odd & there, {"energy": energy, "slab": my_slab + 2 * side - 1}))
+            awaited.append(even & there)
+    for there, target in greeted:
         @pl.when(there)
         def _():
             pl.semaphore_signal(barrier, inc=1, device_id=target, device_id_type=MESH)
 
+    nothing = jnp.zeros((half, LANES), BF16)
     for side in range(2):
-        @pl.when(jnp.logical_not(links[side][0]))
-        def _():
-            arrived[side] = jnp.zeros((half, LANES), BF16)
+        @pl.when(jnp.logical_not(exists[side]))
+        def _():
+            for kind in range(3):
+                arrived[side, kind] = nothing
 
     @pl.when(jnp.logical_not(inside))
     def _():
+        for side in range(2):
+            arrived[side, 2] = nothing
         for group in range(groups):
             halo[2, group] = jnp.zeros((PAIRS, LANES), BF16)
 
@@ -440,18 +451,30 @@
     outgoing[0] = jnp.where(lower, top, pltpu.roll(bottom, middle, 1)).astype(BF16)
     outgoing[1] = jnp.where(lower, pltpu.roll(top, middle, 1), bottom).astype(BF16)
 
-    count = sum(there.astype(jnp.int32) for there, _ in links)
+    count = sum(there.astype(jnp.int32) for there in awaited)
     pl.semaphore_wait(barrier, count)
 
-    def edge_copy(side, slot):
+    def edge_copy(side, kind, slot):
+        energy = (my_energy, my_energy + ahead, beyond)[kind]
         return pltpu.make_async_remote_copy(
             src_ref=outgoing.at[side],
-            dst_ref=arrived.at[slot],
-            send_sem=edge_send.at[side],
-            recv_sem=edge_recv.at[slot],
-            device_id=links[side][1],
+            dst_ref=arrived.at[slot, kind],
+            send_sem=edge_send.at[side, kind],
+            recv_sem=edge_recv.at[slot, kind],
+            device_id={"energy": energy, "slab": my_slab + 2 * side - 1},
             device_id_type=MESH,
         )
+
+    def taking(side, kind, role):
+        there = exists[side] if kind == 0 else exists[side] & role
+        return there if kind < 2 else there & inside
+
+    def awaiting(kinds, role):
+        for kind in kinds:
+            for side in range(2):
+                @pl.when(taking(side, kind, role))
+                def _():
+                    edge_copy(side, kind, side).wait_recv()
 
     def halo_copy(kind, group):
         return pltpu.make_async_remote_copy(
@@ -469,14 +492,15 @@
             dst_ref=halo.at[2, last],
             send_sem=relay_send,
             recv_sem=halo_recv.at[1, last],
-            device_id=links[4][1],
+            device_id={"energy": onward},
             device_id_type=MESH,
         )
 
-    for side in range(2):
-        @pl.when(links[side][0])
-        def _():
-            edge_copy(side, 1 - side).start()
+    for kind in (2, 1, 0):
+        for side in range(2):
+            @pl.when(taking(side, kind, even))
+            def _():
+                edge_copy(side, kind, 1 - side).start()
 
     for group in range(groups):
         load(group, range(group * per, (group + 1) * per))
@@ -520,16 +544,22 @@
 
     partial[...] = dot(lesser[...], mixing[...])
 
-    for side in range(2):
-        @pl.when(links[side][0])
-        def _():
-            edge_copy(side, side).wait_recv()
-
-    crossing = dot(jnp.concatenate([arrived[0], arrived[1]], axis=1), border[...])
-    crossing = jnp.concatenate([crossing[:, 0:span], crossing[:, span:2 * span]], axis=0)
-    mixed = (partial[...] + crossing).astype(BF16)
-    for group in range(groups):
-        halo[0, group] = mixed[:, group * LANES:(group + 1) * LANES]
+    def crossing(kind):
+        value = dot(jnp.concatenate([arrived[0, kind], arrived[1, kind]], axis=1), border[...])
+        return jnp.concatenate([value[:, 0:span], value[:, span:2 * span]], axis=0)
+
+    def settle(mixed):
+        for group in range(groups):
+            halo[0, group] = mixed[:, group * LANES:(group + 1) * LANES].astype(BF16)
+
+    @pl.when(even)
+    def _():
+        awaiting((0,), odd)
+        settle(partial[...] + crossing(0))
+
+    @pl.when(odd)
+    def _():
+        settle(partial[...])
 
     direct = jnp.logical_not(relayed)
 
@@ -582,6 +612,15 @@
     def _():
         relay_copy().start()
 
+    @pl.when(odd)
+    def _():
+        awaiting((0, 1, 2), odd)
+        pieces = [crossing(kind).astype(BF16) for kind in range(3)]
+        for group in range(groups):
+            lanes = slice(group * LANES, (group + 1) * LANES)
+            far = jnp.concatenate([pieces[1][:, lanes], pieces[2][:, lanes]], axis=1)
+            partial[:, lanes] = partial[:, lanes] + dot(pieces[0][:, lanes], own_band[...]) + dot(far, far_band[...])
+
     identity = jnp.where(iota(square, 0) == iota(square, 1), 1.0, 0.0).astype(BF16)
 
     def place_rows(near, group, values):
@@ -609,10 +648,11 @@
         source[group] = source[group] + total.astype(F32)
         place_rows(g_near, group, sandwich(group).astype(BF16))
 
-    for side in range(2):
-        @pl.when(links[side][0])
-        def _():
-            edge_copy(side, 1 - side).wait_send()
+    for kind in range(3):
+        for side in range(2):
+            @pl.when(taking(side, kind, even))
+            def _():
+                edge_copy(side, kind, 1 - side).wait_send()
 
     for group in range(groups):
         halo_copy(0, group).wait_send()
@@ -671,12 +711,12 @@
             pltpu.VMEM((span, span), BF16),
             pltpu.VMEM((2 * LANES, 2 * span), BF16),
             pltpu.VMEM((2, PAIRS // 2, LANES), BF16),
-            pltpu.VMEM((2, PAIRS // 2, LANES), BF16),
+            pltpu.VMEM((2, 3, PAIRS // 2, LANES), BF16),
             pltpu.VMEM((3, groups, PAIRS, LANES), BF16),
             pltpu.VMEM((LANES, LANES), BF16),
             pltpu.VMEM((2 * LANES, LANES), BF16),
-            pltpu.SemaphoreType.DMA((2,)),
-            pltpu.SemaphoreType.DMA((2,)),
+            pltpu.SemaphoreType.DMA((2, 3)),
+            pltpu.SemaphoreType.DMA((2, 3)),
             pltpu.SemaphoreType.DMA((2, groups)),
             pltpu.SemaphoreType.DMA((2, groups)),
             pltpu.SemaphoreType.DMA,

time: 11.5 us -> 10.6 us (0.922)
  the two profiles are of different devices: /device:TPU:1 before, /device:TPU:25 now
where the time goes in v3:
time: 10.6 us; the launch traced here: 10.4 us
  Pallas kernels  9.8 us (92%)
  between operations  0.64 us (6%)
    pallas_call x1, Pallas kernels, on_device_compact(): pl.pallas_call(body, out_shape=(near_shape, near_shape), in_specs=[far] *...  9.12 us
    pallas_call x1, Pallas kernels, on_device_compact(): pl.pallas_call(delivering, out_shape=(shape, shape), in_specs=[vmem] * 2,...  0.68 us

profile of v3, /device:TPU:25, one launch (start us, length us, event | category | flops | bytes accessed | tf_op | source)
XLA Modules:
  0.0 10.4 jit_solution(8991511107281962736)
XLA Ops:
  0.6 9.1 %shard_map.104 = (bf16[32,1152]{1,0:T(8,128)(2,1)S(1)}, bf16[32,1152]{1,0:T(8,128)(2,1)S(1)}) custom-call(bf16[32,1152]{1,0:T(8,128)(2,1)} %green_far.1, bf16[32,1152]{1,0:T(8,128)(2,1)} %sigma_far.1, s32[8,8]{1,0:T(8,128)} %neighbours_far.1, f32[8,8]{1,0:T(8,128)} %coupling_far.1, s32[1,2]{1,0:T(1,128)} %down_far.1, s32[1,2]{1,0:T(1,128)} %up_far.1, ...), custom_call_target="tpu_custom_call" | custom-call | tf_op jit(solution)/shard_map/pallas_call | solution.py:695
  9.8 0.7 %shard_map.105 = (bf16[32,1152]{1,0:T(8,128)(2,1)}, bf16[32,1152]{1,0:T(8,128)(2,1)}) custom-call(bf16[32,1152]{1,0:T(8,128)(2,1)S(1)} %get-tuple-element.4.sigma_near, bf16[32,1152]{1,0:T(8,128)(2,1)S(1)} %get-tuple-element.5.g_near), custom_call_target="tpu_custom_call" | custom-call | tf_op jit(solution)/shard_map/pallas_call | solution.py:728

commit v4 on v3

--- a/solution.py
+++ b/solution.py
@@ -373,7 +373,7 @@
     odd = my_slab % 2 == 1
     even = jnp.logical_not(odd)
     exists = (my_slab > 0, my_slab < slabs - 1)
-    relayed = my_slab == slabs - 1
+    relayed = odd
     beyond = my_energy - ahead
     inside = (beyond >= 0) & (beyond < energies)
     onward, origin = my_energy + 2 * ahead, my_energy - 2 * ahead
@@ -452,15 +452,14 @@
     outgoing[1] = jnp.where(lower, pltpu.roll(top, middle, 1), bottom).astype(BF16)
 
     count = sum(there.astype(jnp.int32) for there in awaited)
-    pl.semaphore_wait(barrier, count)
 
     def edge_copy(side, kind, slot):
         energy = (my_energy, my_energy + ahead, beyond)[kind]
         return pltpu.make_async_remote_copy(
             src_ref=outgoing.at[side],
             dst_ref=arrived.at[slot, kind],
-            send_sem=edge_send.at[side, kind],
-            recv_sem=edge_recv.at[slot, kind],
+            send_sem=edge_send.at[side],
+            recv_sem=edge_recv.at[slot],
             device_id={"energy": energy, "slab": my_slab + 2 * side - 1},
             device_id_type=MESH,
         )
@@ -469,18 +468,32 @@
         there = exists[side] if kind == 0 else exists[side] & role
         return there if kind < 2 else there & inside
 
-    def awaiting(kinds, role):
-        for kind in kinds:
-            for side in range(2):
-                @pl.when(taking(side, kind, role))
-                def _():
-                    edge_copy(side, kind, side).wait_recv()
+    def edge_bytes(side, kinds):
+        return pltpu.make_async_remote_copy(
+            src_ref=arrived.at[side, 0:kinds],
+            dst_ref=arrived.at[side, 0:kinds],
+            send_sem=edge_send.at[side],
+            recv_sem=edge_recv.at[side],
+            device_id={"slab": my_slab + 2 * side - 1},
+            device_id_type=MESH,
+        )
+
+    def counted(side, several, act):
+        there = exists[side]
+        for kinds, when in (
+            (1, there & jnp.logical_not(several)),
+            (2, there & several & jnp.logical_not(inside)),
+            (3, there & several & inside),
+        ):
+            @pl.when(when)
+            def _():
+                act(edge_bytes(side, kinds))
 
     def halo_copy(kind, group):
         return pltpu.make_async_remote_copy(
             src_ref=halo.at[0, group],
             dst_ref=halo.at[1 + kind, group],
-            send_sem=halo_send.at[kind, group],
+            send_sem=halo_send.at[kind],
             recv_sem=halo_recv.at[kind, group],
             device_id=links[2 + kind][1],
             device_id_type=MESH,
@@ -496,16 +509,27 @@
             device_id_type=MESH,
         )
 
-    for kind in (2, 1, 0):
-        for side in range(2):
-            @pl.when(taking(side, kind, even))
-            def _():
-                edge_copy(side, kind, 1 - side).start()
+    @pl.when(even)
+    def _():
+        pl.semaphore_wait(barrier, count)
+        for kind in (2, 1, 0):
+            for side in range(2):
+                @pl.when(taking(side, kind, even))
+                def _():
+                    edge_copy(side, kind, 1 - side).start()
 
     for group in range(groups):
         load(group, range(group * per, (group + 1) * per))
     for group in range(groups):
         lesser[:, group * LANES:(group + 1) * LANES] = sandwich(group).astype(BF16)
+
+    @pl.when(odd)
+    def _():
+        pl.semaphore_wait(barrier, count)
+        for side in (1, 0):
+            @pl.when(exists[side])
+            def _():
+                edge_copy(side, 0, 1 - side).start()
 
     for fetch in fetches[4:]:
         fetch.wait()
@@ -554,7 +578,11 @@
 
     @pl.when(even)
     def _():
-        awaiting((0,), odd)
+        for side in range(2):
+            @pl.when(exists[side])
+            def _():
+                edge_bytes(side, 1).wait_recv()
+
         settle(partial[...] + crossing(0))
 
     @pl.when(odd)
@@ -572,8 +600,8 @@
         def _():
             halo_copy(1, group).start()
 
-        if group < last:
-            halo_copy(0, group).start()
+    for group in range(last):
+        halo_copy(0, group).start()
 
     @pl.when(direct)
     def _():
@@ -614,7 +642,9 @@
 
     @pl.when(odd)
     def _():
-        awaiting((0, 1, 2), odd)
+        for side in range(2):
+            counted(side, odd, lambda copy: copy.wait_recv())
+
         pieces = [crossing(kind).astype(BF16) for kind in range(3)]
         for group in range(groups):
             lanes = slice(group * LANES, (group + 1) * LANES)
@@ -648,18 +678,28 @@
         source[group] = source[group] + total.astype(F32)
         place_rows(g_near, group, sandwich(group).astype(BF16))
 
-    for kind in range(3):
-        for side in range(2):
-            @pl.when(taking(side, kind, even))
-            def _():
-                edge_copy(side, kind, 1 - side).wait_send()
-
-    for group in range(groups):
-        halo_copy(0, group).wait_send()
-
-        @pl.when(inside if group < last else inside & direct)
-        def _():
-            halo_copy(1, group).wait_send()
+    for side in range(2):
+        counted(side, even, lambda copy: copy.wait_send())
+
+    def halo_bytes(kind, count):
+        return pltpu.make_async_remote_copy(
+            src_ref=halo.at[0, 0:count],
+            dst_ref=halo.at[1 + kind, 0:count],
+            send_sem=halo_send.at[kind],
+            recv_sem=halo_recv.at[kind, 0],
+            device_id=links[2 + kind][1],
+            device_id_type=MESH,
+        )
+
+    halo_bytes(0, groups).wait_send()
+
+    @pl.when(inside & direct)
+    def _():
+        halo_bytes(1, groups).wait_send()
+
+    @pl.when(inside & relayed)
+    def _():
+        halo_bytes(1, last).wait_send()
 
     @pl.when(relays)
     def _():
@@ -715,9 +755,9 @@
             pltpu.VMEM((3, groups, PAIRS, LANES), BF16),
             pltpu.VMEM((LANES, LANES), BF16),
             pltpu.VMEM((2 * LANES, LANES), BF16),
-            pltpu.SemaphoreType.DMA((2, 3)),
-            pltpu.SemaphoreType.DMA((2, 3)),
-            pltpu.SemaphoreType.DMA((2, groups)),
+            pltpu.SemaphoreType.DMA((2,)),
+            pltpu.SemaphoreType.DMA((2,)),
+            pltpu.SemaphoreType.DMA((2,)),
             pltpu.SemaphoreType.DMA((2, groups)),
             pltpu.SemaphoreType.DMA,
         ],

time: 10.6 us -> 10.4 us (0.981)
  the two profiles are of different devices: /device:TPU:25 before, /device:TPU:20 now
where the time goes in v4:
time: 10.4 us; the launch traced here: 10.3 us
  Pallas kernels  9.62 us (92%)
  between operations  0.64 us (6%)
    pallas_call x1, Pallas kernels, on_device_compact(): pl.pallas_call(body, out_shape=(near_shape, near_shape), in_specs=[far] *...  8.94 us
    pallas_call x1, Pallas kernels, on_device_compact(): pl.pallas_call(delivering, out_shape=(shape, shape), in_specs=[vmem] * 2,...  0.68 us

profile of v4, /device:TPU:20, one launch (start us, length us, event | category | flops | bytes accessed | tf_op | source)
XLA Modules:
  0.0 10.3 jit_solution(3783312166021440712)
XLA Ops:
  0.6 8.9 %shard_map.104 = (bf16[32,1152]{1,0:T(8,128)(2,1)S(1)}, bf16[32,1152]{1,0:T(8,128)(2,1)S(1)}) custom-call(bf16[32,1152]{1,0:T(8,128)(2,1)} %green_far.1, bf16[32,1152]{1,0:T(8,128)(2,1)} %sigma_far.1, s32[8,8]{1,0:T(8,128)} %neighbours_far.1, f32[8,8]{1,0:T(8,128)} %coupling_far.1, s32[1,2]{1,0:T(1,128)} %down_far.1, s32[1,2]{1,0:T(1,128)} %up_far.1, ...), custom_call_target="tpu_custom_call" | custom-call | tf_op jit(solution)/shard_map/pallas_call | solution.py:735
  9.6 0.7 %shard_map.105 = (bf16[32,1152]{1,0:T(8,128)(2,1)}, bf16[32,1152]{1,0:T(8,128)(2,1)}) custom-call(bf16[32,1152]{1,0:T(8,128)(2,1)S(1)} %get-tuple-element.4.sigma_near, bf16[32,1152]{1,0:T(8,128)(2,1)S(1)} %get-tuple-element.5.g_near), custom_call_target="tpu_custom_call" | custom-call | tf_op jit(solution)/shard_map/pallas_call | solution.py:768

commit v5 on v4

--- a/solution.py
+++ b/solution.py
@@ -578,12 +578,17 @@
 
     @pl.when(even)
     def _():
-        for side in range(2):
+        for side in (1, 0):
             @pl.when(exists[side])
             def _():
                 edge_bytes(side, 1).wait_recv()
 
-        settle(partial[...] + crossing(0))
+            value = dot(arrived[side, 0], border[side * LANES:(side + 1) * LANES, :])
+            value = partial[...] + jnp.concatenate([value[:, 0:span], value[:, span:2 * span]], axis=0)
+            if side == 1:
+                partial[...] = value
+            else:
+                settle(value)
 
     @pl.when(odd)
     def _():

time: 10.4 us -> 10.5 us (level)
  the two profiles are of different devices: /device:TPU:20 before, /device:TPU:0 now
where the time goes in v5:
time: 10.5 us; the launch traced here: 10.3 us
  Pallas kernels  9.7 us (92%)
  between operations  0.64 us (6%)
    pallas_call x1, Pallas kernels, on_device_compact(): pl.pallas_call(body, out_shape=(near_shape, near_shape), in_specs=[far] *...  9.03 us
    pallas_call x1, Pallas kernels, on_device_compact(): pl.pallas_call(delivering, out_shape=(shape, shape), in_specs=[vmem] * 2,...  0.68 us

profile of v5, /device:TPU:0, one launch (start us, length us, event | category | flops | bytes accessed | tf_op | source)
XLA Modules:
  0.0 10.3 jit_solution(3422972910350919419)
XLA Ops:
  0.6 9.0 %shard_map.104 = (bf16[32,1152]{1,0:T(8,128)(2,1)S(1)}, bf16[32,1152]{1,0:T(8,128)(2,1)S(1)}) custom-call(bf16[32,1152]{1,0:T(8,128)(2,1)} %green_far.1, bf16[32,1152]{1,0:T(8,128)(2,1)} %sigma_far.1, s32[8,8]{1,0:T(8,128)} %neighbours_far.1, f32[8,8]{1,0:T(8,128)} %coupling_far.1, s32[1,2]{1,0:T(1,128)} %down_far.1, s32[1,2]{1,0:T(1,128)} %up_far.1, ...), custom_call_target="tpu_custom_call" | custom-call | tf_op jit(solution)/shard_map/pallas_call | solution.py:740
  9.7 0.7 %shard_map.105 = (bf16[32,1152]{1,0:T(8,128)(2,1)}, bf16[32,1152]{1,0:T(8,128)(2,1)}) custom-call(bf16[32,1152]{1,0:T(8,128)(2,1)S(1)} %get-tuple-element.4.sigma_near, bf16[32,1152]{1,0:T(8,128)(2,1)S(1)} %get-tuple-element.5.g_near), custom_call_target="tpu_custom_call" | custom-call | tf_op jit(solution)/shard_map/pallas_call | solution.py:773
